TPU v7x, 32 devices: a whole 2x2x4 slice. The times are simulated.
32 devices in a mesh: seq: 8 (over z, y), head: 4 (over x, core).
Axes of the slice: x: 2, y: 2, z: 4, core: 2. Of those that a mesh axis runs over, the one named last changes fastest.
Arguments:
- q_old: bfloat16 [1792, 2048], P(('seq', 'head')), may hold values from -6 to 6
- k_old: bfloat16 [1792, 1024], P(('seq', 'head')), may hold values from -6 to 6
- value_old_layout: bfloat16 [1792, 1024], P(('seq', 'head')), may hold values from -6 to 6
- dout_old: bfloat16 [1792, 2048], P(('seq', 'head')), may hold values from -6 to 6
- old_offsets: int32 [9], replicated, may hold values from 0 to 1024, as said below
- new_offsets: int32 [9], replicated, may hold values from 0 to 1024, as said below
Outputs:
- attn_out: bfloat16 [1792, 2048], P('seq', 'head')
- grad_query_out: bfloat16 [1792, 2048], P('seq', 'head')
- grad_key_out: bfloat16 [1792, 1024], P('seq', 'head')
- grad_value_out: bfloat16 [1792, 1024], P('seq', 'head')
Inputs may be any that keep to these rules, and one draw needn't show every extreme that they name: old_offsets[0] = 0 and old_offsets[8] = 1024; old_offsets[j] lies within 48 of j * 128, at exactly -48 for some j and +48 for some j; some block has exactly 224 positions. new_offsets[0] = 0 and new_offsets[8] = 1024; new_offsets[j] lies within 48 of j * 128, at exactly -48 for some j and +48 for some j; some block has exactly 224 positions; for some j, 96 positions of old block j lie in new block j + 1, and for some j, 96 positions of old block j lie in new block j - 1.
All inputs are finite; a program needn't handle non-finite values.
Results may differ from a plain program's by a relative error of at most 0.02.
Values may be sent and summed in bfloat16 or wider, within the bound.
A program may use at most 64 MiB of HBM per device.

v0:
```python
import jax
import jax.numpy as jnp
from jax import lax
from jax.sharding import PartitionSpec as P

TOK_DEV = 128
ATTEND_WINDOW = 1024
HEAD_SIZE = 128


query_scale = 168.0 ** (-0.5)


def shifted(value, axis, steps):
    count = lax.axis_size(axis)
    initial, last = (max(0, -steps), min(count, count - steps))
    return lax.ppermute(value, axis, [(source, source + steps) for source in range(initial, last)])


def relocate(row_data, source, target, slot_slack, out_rows):
    device = lax.axis_index("seq")
    own_rows = row_data.shape[0]
    first_row = source[device]
    end_row = source[device + 1]
    tail_start = jnp.maximum(end_row - first_row - slot_slack, 0)
    tail_rows = lax.dynamic_slice_in_dim(row_data, tail_start, slot_slack, 0)
    head_rows = row_data[:slot_slack]
    from_left = shifted(tail_rows, "seq", 1)
    from_right = shifted(head_rows, "seq", -1)
    before_row = source[jnp.maximum(device - 1, 0)]
    left_start = before_row + jnp.maximum(first_row - before_row - slot_slack, 0)
    candidates = jnp.concatenate([from_left, row_data, from_right], axis=0)
    targets = target[device] + jnp.arange(out_rows, dtype=jnp.int32)
    selected = jnp.where(
        targets < first_row,
        targets - left_start,
        jnp.where(
            targets < end_row,
            slot_slack + targets - first_row,
            slot_slack + own_rows + targets - end_row,
        ),
    )
    selected = jnp.clip(selected, 0, candidates.shape[0] - 1)
    is_live = targets < target[device + 1]
    return jnp.where(
        is_live[:, None], jnp.take(candidates, selected, axis=0), jnp.zeros((), row_data.dtype)
    )


def key_window(key_value, farthest, nearest):
    device = lax.axis_index("seq")
    devices = lax.axis_size("seq")
    gathered, places, live_parts = ([], [], [])
    for distance in range(farthest, nearest - 1, -1):
        if distance == 0:
            arrived = key_value
        else:
            arrived = shifted(key_value, "seq", distance)
        source_block = device - distance
        gathered.append(arrived)
        places.append(source_block * TOK_DEV + jnp.arange(TOK_DEV, dtype=jnp.int32))
        live_parts.append(jnp.full((TOK_DEV,), (source_block >= 0) & (source_block < devices)))
    return (jnp.concatenate(gathered, axis=0), jnp.concatenate(places), jnp.concatenate(live_parts))


def return_grads(grads, farthest, nearest):
    summed = None
    for position, distance in enumerate(range(farthest, nearest - 1, -1)):
        block = grads[position * TOK_DEV : (position + 1) * TOK_DEV]
        if distance == 0:
            arrived = block
        else:
            arrived = shifted(block, "seq", -distance)
        summed = arrived if summed is None else summed + arrived
    return summed


def attend(
    queries, grads_out, key_rows, value_rows, query_places, query_live, key_places, key_live
):
    head_count = queries.shape[1] // HEAD_SIZE
    kv_count = key_rows.shape[1] // HEAD_SIZE
    heads_per_group = head_count // kv_count
    gap_rows = query_places[:, None] - key_places[None, :]
    allowed = (gap_rows >= 0) & (gap_rows < ATTEND_WINDOW) & query_live[:, None] & key_live[None, :]
    contract_last = (((1,), (1,)), ((), ()))
    contract_first = (((0,), (0,)), ((), ()))
    attn_parts, query_grads, key_grads, value_grads = ([], [], [], [])
    for kv_head in range(kv_count):
        key_head = key_rows[:, kv_head * HEAD_SIZE : (kv_head + 1) * HEAD_SIZE]
        value_head = value_rows[:, kv_head * HEAD_SIZE : (kv_head + 1) * HEAD_SIZE]
        key_total = jnp.zeros((key_rows.shape[0], HEAD_SIZE), jnp.float32)
        value_total = jnp.zeros((key_rows.shape[0], HEAD_SIZE), jnp.float32)
        for member in range(heads_per_group):
            head_number = kv_head * heads_per_group + member
            query_head = queries[:, head_number * HEAD_SIZE : (head_number + 1) * HEAD_SIZE]
            grad_head = grads_out[:, head_number * HEAD_SIZE : (head_number + 1) * HEAD_SIZE]
            scores = (
                lax.dot_general(
                    query_head, key_head, contract_last, preferred_element_type=jnp.float32
                )
                * query_scale
            )
            scores = jnp.where(allowed, scores, -1e30)
            row_max = jnp.max(scores, axis=1, keepdims=True)
            weights = jnp.where(allowed, jnp.exp(scores - row_max), 0.0)
            row_total = jnp.sum(weights, axis=1, keepdims=True)
            probabilities = weights / jnp.where(query_live[:, None], row_total, 1.0)
            rounded = probabilities.astype(jnp.bfloat16)
            head_out = jnp.dot(rounded, value_head, preferred_element_type=jnp.float32).astype(
                jnp.bfloat16
            )
            row_delta = jnp.sum(
                grad_head.astype(jnp.float32) * head_out.astype(jnp.float32), axis=1, keepdims=True
            )
            grad_prob = lax.dot_general(
                grad_head, value_head, contract_last, preferred_element_type=jnp.float32
            )
            grad_score = (probabilities * (grad_prob - row_delta) * query_scale).astype(
                jnp.bfloat16
            )
            query_grads.append(
                jnp.dot(grad_score, key_head, preferred_element_type=jnp.float32).astype(
                    jnp.bfloat16
                )
            )
            key_total = key_total + lax.dot_general(
                grad_score, query_head, contract_first, preferred_element_type=jnp.float32
            )
            value_total = value_total + lax.dot_general(
                rounded, grad_head, contract_first, preferred_element_type=jnp.float32
            )
            attn_parts.append(head_out)
        key_grads.append(key_total)
        value_grads.append(value_total)
    return (
        jnp.concatenate(attn_parts, axis=1),
        jnp.concatenate(query_grads, axis=1),
        jnp.concatenate(key_grads, axis=1),
        jnp.concatenate(value_grads, axis=1),
    )


def on_device(q_old, k_old, value_old_layout, dout_old, old_offsets, new_offsets):
    query_rows, grad_rows, key_rows, value_rows = (
        lax.all_to_all(q_old, "head", split_axis=1, concat_axis=0, tiled=True),
        lax.all_to_all(dout_old, "head", split_axis=1, concat_axis=0, tiled=True),
        lax.all_to_all(k_old, "head", split_axis=1, concat_axis=0, tiled=True),
        lax.all_to_all(value_old_layout, "head", split_axis=1, concat_axis=0, tiled=True),
    )
    device = lax.axis_index("seq")
    devices = lax.axis_size("seq")
    even_offsets = jnp.arange(devices + 1, dtype=jnp.int32) * TOK_DEV
    query_width = query_rows.shape[1]
    key_width = key_rows.shape[1]
    slot_rows = query_rows.shape[0]
    slot_slack = (slot_rows - TOK_DEV) // 2
    halo_blocks = ATTEND_WINDOW // TOK_DEV
    relocated = relocate(
        jnp.concatenate([query_rows, grad_rows, key_rows, value_rows], axis=1),
        old_offsets,
        even_offsets,
        slot_slack,
        TOK_DEV,
    )
    queries = relocated[:, :query_width]
    grads_out = relocated[:, query_width : 2 * query_width]
    buffered, key_places, key_live = key_window(relocated[:, 2 * query_width :], halo_blocks, 0)
    query_places = device * TOK_DEV + jnp.arange(TOK_DEV, dtype=jnp.int32)
    query_live = jnp.full((TOK_DEV,), True)
    attn, grad_query, key_grad, value_grad = attend(
        queries,
        grads_out,
        buffered[:, :key_width],
        buffered[:, key_width:],
        query_places,
        query_live,
        key_places,
        key_live,
    )
    pair_grads = return_grads(
        jnp.concatenate([key_grad, value_grad], axis=1), halo_blocks, 0
    ).astype(jnp.bfloat16)
    placed = relocate(
        jnp.concatenate([attn, grad_query, pair_grads], axis=1),
        even_offsets,
        new_offsets,
        slot_slack,
        slot_rows,
    )
    attn_out = placed[:, :query_width]
    grad_query_out = placed[:, query_width : 2 * query_width]
    grad_key_out = placed[:, 2 * query_width : 2 * query_width + key_width]
    grad_value_out = placed[:, 2 * query_width + key_width :]
    return (attn_out, grad_query_out, grad_key_out, grad_value_out)


def solution(mesh):
    return jax.shard_map(
        on_device,
        mesh=mesh,
        in_specs=(
            P(("seq", "head"), None),
            P(("seq", "head"), None),
            P(("seq", "head"), None),
            P(("seq", "head"), None),
            P(),
            P(),
        ),
        out_specs=(P("seq", "head"), P("seq", "head"), P("seq", "head"), P("seq", "head")),
        check_vma=False,
    )
```

profile of v0, /device:TPU:0, one launch (start us, length us, event | category | flops | bytes accessed | tf_op | source)
XLA Modules:
  0.0 165.6 jit_solution(6059942181810001337)
XLA Ops:
  0.6 1.6 copy.33
  2.2 4.2 %all-to-all-start.2 = ((bf16[56,4,256]{2,0,1:T(8,128)(2,1)}), bf16[56,4,256]{2,0,1:T(8,128)(2,1)S(1)}, u32[]{:S(2)}, u32[]{:S(2)}) async-start(bf16[56,4,256]{2,0,1:T(8,128)(2,1)} %bitcast.43), calls=%async_computation.2 | async-start | bytes 229376 | tf_op jit(solution)/shard_map/all_to_all | solution.py:148
  6.5 1.4 fusion.94
  12.2 1.6 copy.32
  13.8 1.6 copy.31
  16.2 3.4 %all-to-all-start.3 = ((bf16[56,4,256]{2,0,1:T(8,128)(2,1)}), bf16[56,4,256]{2,0,1:T(8,128)(2,1)S(1)}, u32[]{:S(2)}, u32[]{:S(2)}) async-start(bf16[56,4,256]{2,0,1:T(8,128)(2,1)} %bitcast.42), calls=%async_computation.3 | async-start | bytes 229376 | tf_op jit(solution)/shard_map/all_to_all | solution.py:149
  19.6 4.4 %all-to-all-done.3 = bf16[56,4,256]{2,0,1:T(8,128)(2,1)S(1)} async-done(((bf16[56,4,256]{2,0,1:T(8,128)(2,1)}), bf16[56,4,256]{2,0,1:T(8,128)(2,1)S(1)}, u32[]{:S(2)}, u32[]{:S(2)}) %all-to-all-start.3) | async-done | bytes 114720 | tf_op jit(solution)/shard_map/all_to_all | solution.py:149
  24.0 3.4 %all-to-all-start = ((bf16[56,4,512]{2,0,1:T(8,128)(2,1)}), bf16[56,4,512]{2,0,1:T(8,128)(2,1)S(1)}, u32[]{:S(2)}, u32[]{:S(2)}) async-start(bf16[56,4,512]{2,0,1:T(8,128)(2,1)} %bitcast.41), calls=%async_computation | async-start | bytes 458752 | tf_op jit(solution)/shard_map/all_to_all | solution.py:146
  28.1 5.0 %all-to-all-done = bf16[56,4,512]{2,0,1:T(8,128)(2,1)S(1)} async-done(((bf16[56,4,512]{2,0,1:T(8,128)(2,1)}), bf16[56,4,512]{2,0,1:T(8,128)(2,1)S(1)}, u32[]{:S(2)}, u32[]{:S(2)}) %all-to-all-start) | async-done | bytes 229408 | tf_op jit(solution)/shard_map/all_to_all | solution.py:146
  33.0 3.4 %all-to-all-start.1 = ((bf16[56,4,512]{2,0,1:T(8,128)(2,1)}), bf16[56,4,512]{2,0,1:T(8,128)(2,1)S(1)}, u32[]{:S(2)}, u32[]{:S(2)}) async-start(bf16[56,4,512]{2,0,1:T(8,128)(2,1)} %bitcast.40), calls=%async_computation.1 | async-start | bytes 458752 | tf_op jit(solution)/shard_map/all_to_all | solution.py:147
  36.5 5.6 %all-to-all-done.1 = bf16[56,4,512]{2,0,1:T(8,128)(2,1)S(1)} async-done(((bf16[56,4,512]{2,0,1:T(8,128)(2,1)}), bf16[56,4,512]{2,0,1:T(8,128)(2,1)S(1)}, u32[]{:S(2)}, u32[]{:S(2)}) %all-to-all-start.1) | async-done | bytes 229408 | tf_op jit(solution)/shard_map/all_to_all | solution.py:147
  42.1 4.0 %collective-permute-start = (bf16[48,1536]{1,0:T(8,128)(2,1)S(1)}, bf16[48,1536]{1,0:T(8,128)(2,1)S(1)}, u32[]{:S(2)}, u32[]{:S(2)}) collective-permute-start(bf16[48,1536]{1,0:T(8,128)(2,1)S(1)} %get-tuple-element.24), channel_id=1, source_target_pairs={{0,4},{4,8},{8,12},{12,16},{16,20},{20,24},{24,28},{1,5},{5,9},{9,... | collective-permute-start | bytes 442376 | tf_op jit(solution)/shard_map/ppermute | solution.py:17
  48.9 4.3 %collective-permute-done.1 = bf16[48,1536]{1,0:T(8,128)(2,1)S(1)} collective-permute-done((bf16[48,1536]{1,0:T(8,128)(2,1)S(1)}, bf16[48,1536]{1,0:T(8,128)(2,1)S(1)}, u32[]{:S(2)}, u32[]{:S(2)}) %collective-permute-start.1) | collective-permute-done | bytes 147488 | tf_op jit(solution)/shard_map/ppermute | solution.py:17
  57.8 5.2 %collective-permute-start.3 = (bf16[128,512]{0,1:T(8,128)(2,1)S(1)}, bf16[128,512]{0,1:T(8,128)(2,1)S(1)}, u32[]{:S(2)}, u32[]{:S(2)}) collective-permute-start(bf16[128,512]{0,1:T(8,128)(2,1)S(1)} %slice.134), channel_id=1, source_target_pairs={{0,28},{1,29},{2,30},{3,31}} | collective-permute-start | bytes 393224 | tf_op jit(solution)/shard_map/ppermute | solution.py:17
  64.4 1.9 %collective-permute-start.8 = (bf16[128,512]{0,1:T(8,128)(2,1)S(1)}, bf16[128,512]{0,1:T(8,128)(2,1)S(1)}, u32[]{:S(2)}, u32[]{:S(2)}) collective-permute-start(bf16[128,512]{0,1:T(8,128)(2,1)S(1)} %slice.134), channel_id=1, source_target_pairs={{0,8},{4,12},{8,16},{12,20},{16,24},{20,28},{1,9},{5,13},{9,17},{1... | collective-permute-start | bytes 393224 | tf_op jit(solution)/shard_map/ppermute | solution.py:17
  66.3 4.3 %collective-permute-start.7 = (bf16[128,512]{0,1:T(8,128)(2,1)S(1)}, bf16[128,512]{0,1:T(8,128)(2,1)S(1)}, u32[]{:S(2)}, u32[]{:S(2)}) collective-permute-start(bf16[128,512]{0,1:T(8,128)(2,1)S(1)} %slice.134), channel_id=1, source_target_pairs={{0,12},{4,16},{8,20},{12,24},{16,28},{1,13},{5,17},{9,21},{13,25},... | collective-permute-start | bytes 393224 | tf_op jit(solution)/shard_map/ppermute | solution.py:17
  73.3 4.0 %collective-permute-done.4 = bf16[128,512]{0,1:T(8,128)(2,1)S(1)} collective-permute-done((bf16[128,512]{0,1:T(8,128)(2,1)S(1)}, bf16[128,512]{0,1:T(8,128)(2,1)S(1)}, u32[]{:S(2)}, u32[]{:S(2)}) %collective-permute-start.4) | collective-permute-done | bytes 131104 | tf_op jit(solution)/shard_map/ppermute | solution.py:17
  79.3 1.8 %collective-permute-done.6 = bf16[128,512]{0,1:T(8,128)(2,1)S(1)} collective-permute-done((bf16[128,512]{0,1:T(8,128)(2,1)S(1)}, bf16[128,512]{0,1:T(8,128)(2,1)S(1)}, u32[]{:S(2)}, u32[]{:S(2)}) %collective-permute-start.6) | collective-permute-done | bytes 131104 | tf_op jit(solution)/shard_map/ppermute | solution.py:17
  96.9 11.2 %collective-permute-done.11 = f32[128,512]{0,1:T(8,128)S(1)} collective-permute-done((f32[128,512]{0,1:T(8,128)S(1)}, f32[128,512]{0,1:T(8,128)S(1)}, u32[]{:S(2)}, u32[]{:S(2)}) %collective-permute-start.11) | collective-permute-done | bytes 262176 | tf_op jit(solution)/shard_map/ppermute | solution.py:17
  109.4 1.5 collective-permute-start.12
  112.1 5.2 %collective-permute-done.15 = f32[128,512]{0,1:T(8,128)S(1)} collective-permute-done((f32[128,512]{0,1:T(8,128)S(1)}, f32[128,512]{0,1:T(8,128)S(1)}, u32[]{:S(2)}, u32[]{:S(2)}) %collective-permute-start.15) | collective-permute-done | bytes 262176 | tf_op jit(solution)/shard_map/ppermute | solution.py:17
  117.3 27.8 %collective-permute-done.14 = f32[128,512]{0,1:T(8,128)S(1)} collective-permute-done((f32[128,512]{0,1:T(8,128)S(1)}, f32[128,512]{0,1:T(8,128)S(1)}, u32[]{:S(2)}, u32[]{:S(2)}) %collective-permute-start.14) | collective-permute-done | bytes 262176 | tf_op jit(solution)/shard_map/ppermute | solution.py:17
  145.7 1.3 collective-permute-start.18
  149.6 12.4 %collective-permute-done.18 = bf16[48,1536]{0,1:T(8,128)(2,1)S(1)} collective-permute-done((bf16[48,1536]{0,1:T(8,128)(2,1)S(1)}, bf16[48,1536]{0,1:T(8,128)(2,1)S(1)}, u32[]{:S(2)}, u32[]{:S(2)}) %collective-permute-start.18) | collective-permute-done | bytes 147488 | tf_op jit(solution)/shard_map/ppermute | solution.py:17
  (120 shorter events, 40.8 us)
Async XLA Ops:
  2.2 14.0 %all-to-all-start.2 = ((bf16[56,4,256]{2,0,1:T(8,128)(2,1)}), bf16[56,4,256]{2,0,1:T(8,128)(2,1)S(1)}, u32[]{:S(2)}, u32[]{:S(2)}) async-start(bf16[56,4,256]{2,0,1:T(8,128)(2,1)} %bitcast.43), calls=%async_computation.2 | async-start | bytes 229376 | tf_op jit(solution)/shard_map/all_to_all | solution.py:148
  16.2 7.8 %all-to-all-start.3 = ((bf16[56,4,256]{2,0,1:T(8,128)(2,1)}), bf16[56,4,256]{2,0,1:T(8,128)(2,1)S(1)}, u32[]{:S(2)}, u32[]{:S(2)}) async-start(bf16[56,4,256]{2,0,1:T(8,128)(2,1)} %bitcast.42), calls=%async_computation.3 | async-start | bytes 229376 | tf_op jit(solution)/shard_map/all_to_all | solution.py:149
  24.0 9.0 %all-to-all-start = ((bf16[56,4,512]{2,0,1:T(8,128)(2,1)}), bf16[56,4,512]{2,0,1:T(8,128)(2,1)S(1)}, u32[]{:S(2)}, u32[]{:S(2)}) async-start(bf16[56,4,512]{2,0,1:T(8,128)(2,1)} %bitcast.41), calls=%async_computation | async-start | bytes 458752 | tf_op jit(solution)/shard_map/all_to_all | solution.py:146
  33.0 9.0 %all-to-all-start.1 = ((bf16[56,4,512]{2,0,1:T(8,128)(2,1)}), bf16[56,4,512]{2,0,1:T(8,128)(2,1)S(1)}, u32[]{:S(2)}, u32[]{:S(2)}) async-start(bf16[56,4,512]{2,0,1:T(8,128)(2,1)} %bitcast.40), calls=%async_computation.1 | async-start | bytes 458752 | tf_op jit(solution)/shard_map/all_to_all | solution.py:147
  42.1 6.8 %collective-permute-start = (bf16[48,1536]{1,0:T(8,128)(2,1)S(1)}, bf16[48,1536]{1,0:T(8,128)(2,1)S(1)}, u32[]{:S(2)}, u32[]{:S(2)}) collective-permute-start(bf16[48,1536]{1,0:T(8,128)(2,1)S(1)} %get-tuple-element.24), channel_id=1, source_target_pairs={{0,4},{4,8},{8,12},{12,16},{16,20},{20,24},{24,28},{1,5},{5,9},{9,... | collective-permute-start | bytes 442376 | tf_op jit(solution)/shard_map/ppermute | solution.py:17
  46.1 7.0 %collective-permute-start.1 = (bf16[48,1536]{1,0:T(8,128)(2,1)S(1)}, bf16[48,1536]{1,0:T(8,128)(2,1)S(1)}, u32[]{:S(2)}, u32[]{:S(2)}) collective-permute-start(bf16[48,1536]{1,0:T(8,128)(2,1)S(1)} %get-tuple-element.25), channel_id=1, source_target_pairs={{4,0},{8,4},{12,8},{16,12},{20,16},{24,20},{28,24},{5,1},{9,5},{13... | collective-permute-start | bytes 442376 | tf_op jit(solution)/shard_map/ppermute | solution.py:17
  54.4 16.2 %collective-permute-start.2 = (bf16[128,512]{0,1:T(8,128)(2,1)S(1)}, bf16[128,512]{0,1:T(8,128)(2,1)S(1)}, u32[]{:S(2)}, u32[]{:S(2)}) collective-permute-start(bf16[128,512]{0,1:T(8,128)(2,1)S(1)} %slice.134), channel_id=1, source_target_pairs={} | collective-permute-start | bytes 393224 | tf_op jit(solution)/shard_map/ppermute | solution.py:17
  57.8 14.2 %collective-permute-start.3 = (bf16[128,512]{0,1:T(8,128)(2,1)S(1)}, bf16[128,512]{0,1:T(8,128)(2,1)S(1)}, u32[]{:S(2)}, u32[]{:S(2)}) collective-permute-start(bf16[128,512]{0,1:T(8,128)(2,1)S(1)} %slice.134), channel_id=1, source_target_pairs={{0,28},{1,29},{2,30},{3,31}} | collective-permute-start | bytes 393224 | tf_op jit(solution)/shard_map/ppermute | solution.py:17
  63.1 18.2 %collective-permute-start.9 = (bf16[128,512]{0,1:T(8,128)(2,1)S(1)}, bf16[128,512]{0,1:T(8,128)(2,1)S(1)}, u32[]{:S(2)}, u32[]{:S(2)}) collective-permute-start(bf16[128,512]{0,1:T(8,128)(2,1)S(1)} %slice.134), channel_id=1, source_target_pairs={{0,4},{4,8},{8,12},{12,16},{16,20},{20,24},{24,28},{1,5},{5,9},{9,... | collective-permute-start | bytes 393224 | tf_op jit(solution)/shard_map/ppermute | solution.py:17
  64.4 16.8 %collective-permute-start.8 = (bf16[128,512]{0,1:T(8,128)(2,1)S(1)}, bf16[128,512]{0,1:T(8,128)(2,1)S(1)}, u32[]{:S(2)}, u32[]{:S(2)}) collective-permute-start(bf16[128,512]{0,1:T(8,128)(2,1)S(1)} %slice.134), channel_id=1, source_target_pairs={{0,8},{4,12},{8,16},{12,20},{16,24},{20,28},{1,9},{5,13},{9,17},{1... | collective-permute-start | bytes 393224 | tf_op jit(solution)/shard_map/ppermute | solution.py:17
  66.3 14.8 %collective-permute-start.7 = (bf16[128,512]{0,1:T(8,128)(2,1)S(1)}, bf16[128,512]{0,1:T(8,128)(2,1)S(1)}, u32[]{:S(2)}, u32[]{:S(2)}) collective-permute-start(bf16[128,512]{0,1:T(8,128)(2,1)S(1)} %slice.134), channel_id=1, source_target_pairs={{0,12},{4,16},{8,20},{12,24},{16,28},{1,13},{5,17},{9,21},{13,25},... | collective-permute-start | bytes 393224 | tf_op jit(solution)/shard_map/ppermute | solution.py:17
  70.7 6.7 %collective-permute-start.4 = (bf16[128,512]{0,1:T(8,128)(2,1)S(1)}, bf16[128,512]{0,1:T(8,128)(2,1)S(1)}, u32[]{:S(2)}, u32[]{:S(2)}) collective-permute-start(bf16[128,512]{0,1:T(8,128)(2,1)S(1)} %slice.134), channel_id=1, source_target_pairs={{0,24},{4,28},{1,25},{5,29},{2,26},{6,30},{3,27},{7,31}} | collective-permute-start | bytes 393224 | tf_op jit(solution)/shard_map/ppermute | solution.py:17
  72.0 7.3 %collective-permute-start.5 = (bf16[128,512]{0,1:T(8,128)(2,1)S(1)}, bf16[128,512]{0,1:T(8,128)(2,1)S(1)}, u32[]{:S(2)}, u32[]{:S(2)}) collective-permute-start(bf16[128,512]{0,1:T(8,128)(2,1)S(1)} %slice.134), channel_id=1, source_target_pairs={{0,20},{4,24},{8,28},{1,21},{5,25},{9,29},{2,22},{6,26},{10,30},{3... | collective-permute-start | bytes 393224 | tf_op jit(solution)/shard_map/ppermute | solution.py:17
  77.3 3.8 %collective-permute-start.6 = (bf16[128,512]{0,1:T(8,128)(2,1)S(1)}, bf16[128,512]{0,1:T(8,128)(2,1)S(1)}, u32[]{:S(2)}, u32[]{:S(2)}) collective-permute-start(bf16[128,512]{0,1:T(8,128)(2,1)S(1)} %slice.134), channel_id=1, source_target_pairs={{0,16},{4,20},{8,24},{12,28},{1,17},{5,21},{9,25},{13,29},{2,18},{... | collective-permute-start | bytes 393224 | tf_op jit(solution)/shard_map/ppermute | solution.py:17
  89.9 18.2 %collective-permute-start.11 = (f32[128,512]{0,1:T(8,128)S(1)}, f32[128,512]{0,1:T(8,128)S(1)}, u32[]{:S(2)}, u32[]{:S(2)}) collective-permute-start(f32[128,512]{0,1:T(8,128)S(1)} %get-tuple-element.12), channel_id=1, source_target_pairs={{28,0},{29,1},{30,2},{31,3}} | collective-permute-start | bytes 786440 | tf_op jit(solution)/shard_map/ppermute | solution.py:17
  91.2 18.2 %collective-permute-start.17 = (f32[128,512]{0,1:T(8,128)S(1)}, f32[128,512]{0,1:T(8,128)S(1)}, u32[]{:S(2)}, u32[]{:S(2)}) collective-permute-start(f32[128,512]{0,1:T(8,128)S(1)} %get-tuple-element.13), channel_id=1, source_target_pairs={{4,0},{8,4},{12,8},{16,12},{20,16},{24,20},{28,24},{5,1},{9,5},{13... | collective-permute-start | bytes 786440 | tf_op jit(solution)/shard_map/ppermute | solution.py:17
  92.5 18.4 %collective-permute-start.16 = (f32[128,512]{0,1:T(8,128)S(1)}, f32[128,512]{0,1:T(8,128)S(1)}, u32[]{:S(2)}, u32[]{:S(2)}) collective-permute-start(f32[128,512]{0,1:T(8,128)S(1)} %get-tuple-element.14), channel_id=1, source_target_pairs={{8,0},{12,4},{16,8},{20,12},{24,16},{28,20},{9,1},{13,5},{17,9},{2... | collective-permute-start | bytes 786440 | tf_op jit(solution)/shard_map/ppermute | solution.py:17
  94.1 23.2 %collective-permute-start.15 = (f32[128,512]{0,1:T(8,128)S(1)}, f32[128,512]{0,1:T(8,128)S(1)}, u32[]{:S(2)}, u32[]{:S(2)}) collective-permute-start(f32[128,512]{0,1:T(8,128)S(1)} %get-tuple-element.15), channel_id=1, source_target_pairs={{12,0},{16,4},{20,8},{24,12},{28,16},{13,1},{17,5},{21,9},{25,13},... | collective-permute-start | bytes 786440 | tf_op jit(solution)/shard_map/ppermute | solution.py:17
  95.4 49.7 %collective-permute-start.14 = (f32[128,512]{0,1:T(8,128)S(1)}, f32[128,512]{0,1:T(8,128)S(1)}, u32[]{:S(2)}, u32[]{:S(2)}) collective-permute-start(f32[128,512]{0,1:T(8,128)S(1)} %get-tuple-element.16), channel_id=1, source_target_pairs={{16,0},{20,4},{24,8},{28,12},{17,1},{21,5},{25,9},{29,13},{18,2},{... | collective-permute-start | bytes 786440 | tf_op jit(solution)/shard_map/ppermute | solution.py:17
  108.1 37.3 %collective-permute-start.13 = (f32[128,512]{0,1:T(8,128)S(1)}, f32[128,512]{0,1:T(8,128)S(1)}, u32[]{:S(2)}, u32[]{:S(2)}) collective-permute-start(f32[128,512]{0,1:T(8,128)S(1)} %get-tuple-element.17), channel_id=1, source_target_pairs={{20,0},{24,4},{28,8},{21,1},{25,5},{29,9},{22,2},{26,6},{30,10},{2... | collective-permute-start | bytes 786440 | tf_op jit(solution)/shard_map/ppermute | solution.py:17
  109.4 36.0 %collective-permute-start.12 = (f32[128,512]{0,1:T(8,128)S(1)}, f32[128,512]{0,1:T(8,128)S(1)}, u32[]{:S(2)}, u32[]{:S(2)}) collective-permute-start(f32[128,512]{0,1:T(8,128)S(1)} %get-tuple-element.18), channel_id=1, source_target_pairs={{24,0},{28,4},{25,1},{29,5},{26,2},{30,6},{27,3},{31,7}} | collective-permute-start | bytes 786440 | tf_op jit(solution)/shard_map/ppermute | solution.py:17
  110.9 34.5 %collective-permute-start.10 = (f32[128,512]{0,1:T(8,128)S(1)}, f32[128,512]{0,1:T(8,128)S(1)}, u32[]{:S(2)}, u32[]{:S(2)}) collective-permute-start(f32[128,512]{0,1:T(8,128)S(1)} %get-tuple-element.19), channel_id=1, source_target_pairs={} | collective-permute-start | bytes 786440 | tf_op jit(solution)/shard_map/ppermute | solution.py:17
  145.7 16.3 %collective-permute-start.18 = (bf16[48,1536]{0,1:T(8,128)(2,1)S(1)}, bf16[48,1536]{0,1:T(8,128)(2,1)S(1)}, u32[]{:S(2)}, u32[]{:S(2)}) collective-permute-start(bf16[48,1536]{0,1:T(8,128)(2,1)S(1)} %get-tuple-element.26), channel_id=1, source_target_pairs={{0,4},{4,8},{8,12},{12,16},{16,20},{20,24},{24,28},{1,5},{5,9},{9,... | collective-permute-start | bytes 442376 | tf_op jit(solution)/shard_map/ppermute | solution.py:17
  147.0 15.0 %collective-permute-start.19 = (bf16[48,1536]{0,1:T(8,128)(2,1)S(1)}, bf16[48,1536]{0,1:T(8,128)(2,1)S(1)}, u32[]{:S(2)}, u32[]{:S(2)}) collective-permute-start(bf16[48,1536]{0,1:T(8,128)(2,1)S(1)} %get-tuple-element.27), channel_id=1, source_target_pairs={{4,0},{8,4},{12,8},{16,12},{20,16},{24,20},{28,24},{5,1},{9,5},{13... | collective-permute-start | bytes 442376 | tf_op jit(solution)/shard_map/ppermute | solution.py:17
  (1 other events, 14.8 us)
where the time goes:
time: 167 us; the launch traced here: 166 us
  waiting for transfers between devices  82.8 us (50%)
  starting transfers between devices  49.5 us (30%)
  local copies, waits for them, and re-layouts  13.6 us (8%)
  matrix products  7.91 us (5%)
  other arithmetic  7.34 us (4%)
  between operations  4.51 us (3%)
    ppermute x20, waiting for transfers between devices, shifted(): lax.ppermute(value, axis, [(source, source + steps) for source in range(i...  67.8 us
    ppermute x20, starting transfers between devices, shifted(): lax.ppermute(value, axis, [(source, source + steps) for source in range(i...  35.1 us
    all_to_all x1, waiting for transfers between devices, on_device(): lax.all_to_all(dout_old, 'head', split_axis=1, concat_axis=0, tiled=True)  5.59 us
    all_to_all x1, waiting for transfers between devices, on_device(): lax.all_to_all(q_old, 'head', split_axis=1, concat_axis=0, tiled=True)  4.95 us
    all_to_all x1, waiting for transfers between devices, on_device(): lax.all_to_all(value_old_layout, 'head', split_axis=1, concat_axis=0, til...  4.42 us
    all_to_all x1, starting transfers between devices, on_device(): lax.all_to_all(k_old, 'head', split_axis=1, concat_axis=0, tiled=True)  4.24 us
    all_to_all x1, starting transfers between devices, on_device(): lax.all_to_all(q_old, 'head', split_axis=1, concat_axis=0, tiled=True)  3.39 us
    all_to_all x1, starting transfers between devices, on_device(): lax.all_to_all(dout_old, 'head', split_axis=1, concat_axis=0, tiled=True)  3.39 us
  transfers between devices with their start and end apart: 24, of which 13 were waited for; matrix products, arithmetic and copies ran while one was open for 8% of the time, Pallas kernels for 0%

commit v1 on v0

--- a/solution.py
+++ b/solution.py
@@ -1,6 +1,10 @@
+import functools
+
 import jax
 import jax.numpy as jnp
 from jax import lax
+from jax.experimental import pallas as pl
+from jax.experimental.pallas import tpu as pltpu
 from jax.sharding import PartitionSpec as P
 
 TOK_DEV = 128
@@ -195,9 +199,397 @@
     return (attn_out, grad_query_out, grad_key_out, grad_value_out)
 
 
+def joint_kernel(levels, pair, groups, members, *refs):
+    (old_offsets, new_offsets, q_in, k_in, v_in, d_in, attn_out, dq_out, dk_out, dv_out,
+     kv_chunks, qd_chunks, wide, kv_wide, qd_wide, kv_halo, qd_halo, keys, values, queries, grads,
+     probs, grad_probs, grad_send, grad_recv, grad_own, attn_t, dq_t, row_buf, grad_buf, row_ext,
+     grad_ext, in_send, in_recv, in_local, halo_send, halo_recv, cast_send, cast_recv, ret_send,
+     ret_recv, out_send, out_recv, out_local) = refs
+    seq, column = lax.axis_index("seq"), lax.axis_index("head")
+    level, part = seq // pair, seq % pair
+    crowd = pair * groups
+    me = part * groups + column
+    chunk = k_in.shape[0]
+    slots = chunk * groups
+    slack = (slots - TOK_DEV) // 2
+    rows = pair * TOK_DEV
+    width = members * HEAD_SIZE
+    f32, bf16 = jnp.float32, jnp.bfloat16
+
+    def at(to_level, to_part, to_column):
+        return {"seq": to_level * pair + to_part, "head": to_column}
+
+    def send(src, dst, ssem, rsem, where):
+        return pltpu.make_async_remote_copy(
+            src_ref=src, dst_ref=dst, send_sem=ssem, recv_sem=rsem, device_id=where,
+            device_id_type=pl.DeviceIdType.MESH)
+
+    here = at(level, part, column)
+
+    def landed(dst, rsem):
+        send(dst, dst, rsem, rsem, here).wait_recv()
+
+    def left(src, ssem):
+        send(src, src, ssem, ssem, here).wait_send()
+
+    barrier = pltpu.get_barrier_semaphore()
+    for step in range(1, crowd):
+        peer = lax.rem(me + step, crowd)
+        pl.semaphore_signal(barrier, inc=1, device_id=at(level, peer // groups, peer % groups),
+                            device_id_type=pl.DeviceIdType.MESH)
+    for step in range(1, levels):
+        for other in range(pair):
+            pl.semaphore_signal(barrier, inc=1, device_id=at(lax.rem(level + step, levels), other, column),
+                                device_id_type=pl.DeviceIdType.MESH)
+    pl.semaphore_wait(barrier, crowd - 1 + (levels - 1) * pair)
+
+    def pieces(owner, source):
+        head = (owner % groups) * pair + owner // groups
+        k_at = pl.ds(pl.multiple_of(head * HEAD_SIZE, HEAD_SIZE), HEAD_SIZE)
+        q_at = pl.ds(pl.multiple_of(head * width, HEAD_SIZE), width)
+        return (
+            (k_in.at[:, k_at], kv_chunks.at[source, :, pl.ds(0, HEAD_SIZE)]),
+            (v_in.at[:, k_at], kv_chunks.at[source, :, pl.ds(HEAD_SIZE, HEAD_SIZE)]),
+            (q_in.at[:, q_at], qd_chunks.at[source, :, pl.ds(0, width)]),
+            (d_in.at[:, q_at], qd_chunks.at[source, :, pl.ds(width, width)]),
+        )
+
+    for kinds in ((0, 1), (2, 3)):
+        for step in range(crowd):
+            peer = lax.rem(me + step, crowd)
+            for kind in kinds:
+                src, dst = pieces(peer, me)[kind]
+                if step == 0:
+                    pltpu.make_async_copy(src, dst, in_local.at[kind]).start()
+                else:
+                    send(src, dst, in_send.at[kind, step], in_recv.at[kind, step],
+                         at(level, peer // groups, peer % groups)).start()
+
+    def arrive(kinds):
+        for kind in kinds:
+            src, dst = pieces(me, me)[kind]
+            pltpu.make_async_copy(src, dst, in_local.at[kind]).wait()
+            for step in range(1, crowd):
+                source = lax.rem(me + crowd - step, crowd)
+                landed(pieces(me, source)[kind][1], in_recv.at[kind, step])
+
+    def spread(chunks, target):
+        count = chunks.shape[2]
+        wide[:, pl.ds(0, count)] = jnp.zeros((rows + 2 * slack, count), f32)
+        row = lax.broadcasted_iota(jnp.int32, (slots, chunk), 0)
+        slot = lax.broadcasted_iota(jnp.int32, (slots, chunk), 1)
+        for other in range(pair):
+            block = level * pair + other
+            first, end = old_offsets[block], old_offsets[block + 1]
+            total = jnp.zeros((slots, count), f32)
+            for piece in range(groups):
+                place = slot + (first + piece * chunk)
+                pick = (row + (block * TOK_DEV - slack) == place) & (place < end)
+                total = total + jnp.dot(jnp.where(pick, 1.0, 0.0).astype(bf16),
+                                        chunks[other * groups + piece], preferred_element_type=f32)
+            span = pl.ds(other * TOK_DEV, slots)
+            wide[span, pl.ds(0, count)] = wide[span, pl.ds(0, count)] + total
+        target[...] = wide[:, pl.ds(0, count)].astype(bf16)
+
+    def halo(kind, source, dest):
+        down = (source.at[pl.ds(0, slack)], dest.at[1])
+        up = (source.at[pl.ds(rows + slack, slack)], dest.at[0])
+
+        @pl.when(level > 0)
+        def _():
+            send(*down, halo_send.at[kind, 1], halo_recv.at[kind, 1], at(level - 1, part, column)).start()
+
+        @pl.when(level < levels - 1)
+        def _():
+            send(*up, halo_send.at[kind, 0], halo_recv.at[kind, 0], at(level + 1, part, column)).start()
+
+        @pl.when(level > 0)
+        def _():
+            landed(dest.at[0], halo_recv.at[kind, 0])
+
+        @pl.when(level == 0)
+        def _():
+            dest[0] = jnp.zeros(dest.shape[1:], bf16)
+
+        @pl.when(level < levels - 1)
+        def _():
+            landed(dest.at[1], halo_recv.at[kind, 1])
+
+        @pl.when(level == levels - 1)
+        def _():
+            dest[1] = jnp.zeros(dest.shape[1:], bf16)
+
+        return jnp.concatenate([
+            source[pl.ds(slack, slack)] + dest[0],
+            source[pl.ds(2 * slack, rows - 2 * slack)],
+            source[pl.ds(rows, slack)] + dest[1],
+        ], axis=0)
+
+    arrive((0, 1))
+    spread(kv_chunks, kv_wide)
+    block = halo(0, kv_wide, kv_halo)
+    keys[level] = block[:, :HEAD_SIZE]
+    values[level] = block[:, HEAD_SIZE:]
+    for kind, held in ((0, keys), (1, values)):
+        for step in range(1, levels):
+            @pl.when(level + step < levels)
+            def _():
+                send(held.at[level], held.at[level], cast_send.at[kind, step],
+                     cast_recv.at[kind, step], at(level + step, part, column)).start()
+
+    arrive((2, 3))
+    spread(qd_chunks, qd_wide)
+    block = halo(1, qd_wide, qd_halo)
+    for member in range(members):
+        span = pl.ds(member * rows, rows)
+        queries[span] = block[:, member * HEAD_SIZE:(member + 1) * HEAD_SIZE]
+        grads[span] = block[:, width + member * HEAD_SIZE:width + (member + 1) * HEAD_SIZE]
+
+    nt = (((1,), (1,)), ((), ()))
+    tn = (((0,), (0,)), ((), ()))
+    lanes = members * rows
+
+    def score_step(step, row_max):
+        @pl.when(step > 0)
+        def _():
+            landed(keys.at[level - step], cast_recv.at[0, step])
+
+        score = lax.dot_general(keys[level - step], queries[...], nt, preferred_element_type=f32) * query_scale
+        key_place = lax.broadcasted_iota(jnp.int32, (rows, rows), 0)
+        query_place = lax.broadcasted_iota(jnp.int32, (rows, rows), 1) + step * rows
+        allowed = jnp.concatenate([key_place <= query_place] * members, axis=1)
+        score = jnp.where(allowed, score, -1e30)
+        probs[level - step] = score
+        return jnp.maximum(row_max, jnp.max(score, axis=0, keepdims=True))
+
+    row_max = lax.fori_loop(0, level + 1, score_step, jnp.full((1, lanes), -1e30, f32))
+
+    def weight_step(step, total):
+        weight = jnp.exp(probs[step] - row_max)
+        probs[step] = weight
+        return total + jnp.sum(weight, axis=0, keepdims=True)
+
+    row_total = lax.fori_loop(0, level + 1, weight_step, jnp.zeros((1, lanes), f32))
+    inverse = 1.0 / row_total
+    attn_t[...] = jnp.zeros_like(attn_t)
+
+    def value_step(step, carry):
+        @pl.when(step > 0)
+        def _():
+            landed(values.at[level - step], cast_recv.at[1, step])
+
+        prob = probs[level - step] * inverse
+        probs[level - step] = prob
+        attn_t[...] += lax.dot_general(values[level - step], prob.astype(bf16), tn, preferred_element_type=f32)
+        grad_probs[level - step] = lax.dot_general(values[level - step], grads[...], nt, preferred_element_type=f32)
+        return carry
+
+    lax.fori_loop(0, level + 1, value_step, 0)
+    attn = attn_t[...].astype(bf16).astype(f32)
+    delta = jnp.sum(attn * jnp.transpose(grads[...].astype(f32)), axis=0, keepdims=True)
+    attn = jnp.transpose(attn).astype(bf16)
+    dq_t[...] = jnp.zeros_like(dq_t)
+
+    def grad_step(low, carry):
+        prob = probs[low]
+        change = (prob * (grad_probs[low] - delta) * query_scale).astype(bf16)
+        dq_t[...] += lax.dot_general(keys[low], change, tn, preferred_element_type=f32)
+        dk = jnp.dot(change, queries[...], preferred_element_type=f32)
+        dv = jnp.dot(prob.astype(bf16), grads[...], preferred_element_type=f32)
+
+        @pl.when(low < level)
+        def _():
+            grad_send[low] = jnp.concatenate([dk, dv], axis=1).astype(bf16)
+            send(grad_send.at[low], grad_recv.at[level - low], ret_send.at[level - low],
+                 ret_recv.at[level - low], at(low, part, column)).start()
+
+        @pl.when(low == level)
+        def _():
+            grad_own[...] = jnp.concatenate([dk, dv], axis=1)
+
+        return carry
+
+    lax.fori_loop(0, level + 1, grad_step, 0)
+    dq = jnp.transpose(dq_t[...]).astype(bf16)
+    for member in range(members):
+        span = slice(member * rows, (member + 1) * rows)
+        row_buf[:, pl.ds(member * HEAD_SIZE, HEAD_SIZE)] = attn[span]
+        row_buf[:, pl.ds(width + member * HEAD_SIZE, HEAD_SIZE)] = dq[span]
+
+    def routes(other):
+        begin = other * TOK_DEV - slack
+        low, high = max(0, begin), min(rows, begin + slots)
+        return pl.ds(low, high - low), pl.ds(low - begin, high - low)
+
+    head_span, tail_span = pl.ds(0, slack), pl.ds(slots - slack, slack)
+    last_span = pl.ds(rows - slack, slack)
+
+    def hand_out(kind, source, dest):
+        for other in range(pair):
+            take, put = routes(other)
+
+            @pl.when(part == other)
+            def _():
+                pltpu.make_async_copy(source.at[take], dest.at[part, put], out_local.at[kind]).start()
+
+            @pl.when(part != other)
+            def _():
+                send(source.at[take], dest.at[part, put], out_send.at[kind, other],
+                     out_recv.at[kind, part, 0], at(level, other, column)).start()
+
+        @pl.when(level < levels - 1)
+        def _():
+            send(source.at[last_span], dest.at[part, head_span], out_send.at[kind, pair],
+                 out_recv.at[kind, part, 1], at(level + 1, 0, column)).start()
+
+        @pl.when(level > 0)
+        def _():
+            send(source.at[head_span], dest.at[part, tail_span], out_send.at[kind, pair + 1],
+                 out_recv.at[kind, part, 2], at(level - 1, pair - 1, column)).start()
+
+    def take_in(kind, source, dest, place):
+        for other in range(pair):
+            take, put = routes(other)
+
+            @pl.when(part == other)
+            def _():
+                pltpu.make_async_copy(source.at[take], dest.at[part, put], out_local.at[kind]).wait()
+                for giver in range(pair):
+                    if giver != other:
+                        landed(dest.at[giver, put], out_recv.at[kind, giver, 0])
+
+            @pl.when(part != other)
+            def _():
+                left(source.at[take], out_send.at[kind, other])
+
+        for giver in range(pair):
+            @pl.when((part == 0) & (level > 0))
+            def _():
+                landed(dest.at[giver, head_span], out_recv.at[kind, giver, 1])
+
+            @pl.when((part == 0) & (level == 0))
+            def _():
+                dest[giver, head_span] = jnp.zeros((slack, dest.shape[2]), bf16)
+
+            @pl.when((part == pair - 1) & (level < levels - 1))
+            def _():
+                landed(dest.at[giver, tail_span], out_recv.at[kind, giver, 2])
+
+            @pl.when((part == pair - 1) & (level == levels - 1))
+            def _():
+                dest[giver, tail_span] = jnp.zeros((slack, dest.shape[2]), bf16)
+
+        @pl.when(level < levels - 1)
+        def _():
+            left(source.at[last_span], out_send.at[kind, pair])
+
+        @pl.when(level > 0)
+        def _():
+            left(source.at[head_span], out_send.at[kind, pair + 1])
+
+        first, end = new_offsets[seq], new_offsets[seq + 1]
+        slot = lax.broadcasted_iota(jnp.int32, (slots, slots), 0) + first
+        held = lax.broadcasted_iota(jnp.int32, (slots, slots), 1) + (seq * TOK_DEV - slack)
+        pick = jnp.where((slot == held) & (slot < end), 1.0, 0.0).astype(bf16)
+        for giver in range(pair):
+            placed = jnp.dot(pick, dest[giver], preferred_element_type=f32).astype(bf16)
+            for index, out in enumerate(place):
+                count = dest.shape[2] // 2
+                out[:, pl.ds(giver * count, count)] = placed[:, index * count:(index + 1) * count]
+
+    hand_out(0, row_buf, row_ext)
+    for step in range(1, levels):
+        @pl.when(level + step < levels)
+        def _():
+            landed(grad_recv.at[step], ret_recv.at[step])
+            grad_own[...] += grad_recv[step].astype(f32)
+    grad_buf[...] = grad_own[...].astype(bf16)
+    hand_out(1, grad_buf, grad_ext)
+    take_in(0, row_buf, row_ext, (attn_out, dq_out))
+    take_in(1, grad_buf, grad_ext, (dk_out, dv_out))
+
+    for kind in range(4):
+        for step in range(1, crowd):
+            left(pieces(me, me)[kind][0], in_send.at[kind, step])
+    for kind, source in ((0, kv_wide), (1, qd_wide)):
+        @pl.when(level > 0)
+        def _():
+            left(source.at[pl.ds(0, slack)], halo_send.at[kind, 1])
+
+        @pl.when(level < levels - 1)
+        def _():
+            left(source.at[pl.ds(rows + slack, slack)], halo_send.at[kind, 0])
+    for step in range(1, levels):
+        for kind, held in ((0, keys), (1, values)):
+            @pl.when(level + step < levels)
+            def _():
+                left(held.at[level], cast_send.at[kind, step])
+
+        @pl.when(level >= step)
+        def _():
+            left(grad_send.at[level - step], ret_send.at[step])
+
+
+def joint(sequence, groups, q_old, k_old, value_old_layout, dout_old, old_offsets, new_offsets):
+    chunk = q_old.shape[0]
+    pair = k_old.shape[1] // (groups * HEAD_SIZE)
+    members = q_old.shape[1] // k_old.shape[1]
+    levels = sequence // pair
+    slots = chunk * groups
+    slack = (slots - TOK_DEV) // 2
+    rows = pair * TOK_DEV
+    width = members * HEAD_SIZE
+    lanes = members * rows
+    bf16, f32 = jnp.bfloat16, jnp.float32
+    vmem, dma = pltpu.VMEM, pltpu.SemaphoreType.DMA
+    out = lambda count: jax.ShapeDtypeStruct((slots, count), bf16)
+    smem = pl.BlockSpec(memory_space=pltpu.SMEM)
+    anywhere = pl.BlockSpec(memory_space=pl.ANY)
+    whole = pl.BlockSpec(memory_space=pltpu.VMEM)
+    return pl.pallas_call(
+        functools.partial(joint_kernel, levels, pair, groups, members),
+        out_shape=(out(pair * width), out(pair * width), out(pair * HEAD_SIZE), out(pair * HEAD_SIZE)),
+        in_specs=[smem, smem, anywhere, anywhere, anywhere, anywhere],
+        out_specs=(whole,) * 4,
+        scratch_shapes=[
+            vmem((pair * groups, chunk, 2 * HEAD_SIZE), bf16),
+            vmem((pair * groups, chunk, 2 * width), bf16),
+            vmem((rows + 2 * slack, 2 * width), f32),
+            vmem((rows + 2 * slack, 2 * HEAD_SIZE), bf16),
+            vmem((rows + 2 * slack, 2 * width), bf16),
+            vmem((2, slack, 2 * HEAD_SIZE), bf16),
+            vmem((2, slack, 2 * width), bf16),
+            vmem((levels, rows, HEAD_SIZE), bf16),
+            vmem((levels, rows, HEAD_SIZE), bf16),
+            vmem((lanes, HEAD_SIZE), bf16),
+            vmem((lanes, HEAD_SIZE), bf16),
+            vmem((levels, rows, lanes), f32),
+            vmem((levels, rows, lanes), f32),
+            vmem((levels, rows, 2 * HEAD_SIZE), bf16),
+            vmem((levels, rows, 2 * HEAD_SIZE), bf16),
+            vmem((rows, 2 * HEAD_SIZE), f32),
+            vmem((HEAD_SIZE, lanes), f32),
+            vmem((HEAD_SIZE, lanes), f32),
+            vmem((rows, 2 * width), bf16),
+            vmem((rows, 2 * HEAD_SIZE), bf16),
+            vmem((pair, slots, 2 * width), bf16),
+            vmem((pair, slots, 2 * HEAD_SIZE), bf16),
+            dma((4, pair * groups)), dma((4, pair * groups)), dma((4,)),
+            dma((2, 2)), dma((2, 2)),
+            dma((2, levels)), dma((2, levels)),
+            dma((levels,)), dma((levels,)),
+            dma((2, pair + 2)), dma((2, pair, 3)), dma((2,)),
+        ],
+        compiler_params=pltpu.CompilerParams(collective_id=0, has_side_effects=True),
+    )(old_offsets, new_offsets, q_old, k_old, value_old_layout, dout_old)
+
+
 def solution(mesh):
+    sequence, groups = mesh.shape["seq"], mesh.shape["head"]
+    covered = sequence * TOK_DEV <= ATTEND_WINDOW
+    body = functools.partial(joint, sequence, groups) if covered else on_device
     return jax.shard_map(
-        on_device,
+        body,
         mesh=mesh,
         in_specs=(
             P(("seq", "head"), None),

time: 167 us -> 53.7 us (0.32)
  waiting for transfers between devices: 82.8 us -> 0 us
  starting transfers between devices: 49.5 us -> 0 us
  Pallas kernels: 0 us -> 48.2 us
  local copies, waits for them, and re-layouts: 13.6 us -> 4.25 us
  matrix products: 7.91 us -> 0 us
  other arithmetic: 7.34 us -> 0 us
  between operations: 4.51 us -> 0.65 us
    ppermute x20 -> x0, waiting for transfers between devices: 67.8 us -> none  [shifted(): lax.ppermute(value, axis, [(source, source + steps) for source in range(i...]
    pallas_call x0 -> x1, Pallas kernels: none -> 48.2 us  [joint(): pl.pallas_call(functools.partial(joint_kernel, levels, pair, groups, memb...]
    ppermute x20 -> x0, starting transfers between devices: 35.1 us -> none  [shifted(): lax.ppermute(value, axis, [(source, source + steps) for source in range(i...]
    all_to_all x4 -> x0, waiting for transfers between devices: 15 us -> none  [the longest x1 5.59 us: on_device(): lax.all_to_all(dout_old, 'head', split_axis=1, concat_axis=0, tiled=True)]
    all_to_all x4 -> x0, starting transfers between devices: 14.4 us -> none  [the longest x1 4.24 us: on_device(): lax.all_to_all(k_old, 'head', split_axis=1, concat_axis=0, tiled=True)]
    dot_general x24 -> x0, matrix products: 7.91 us -> none  [the longest x4 1.73 us: attend(): lax.dot_general(query_head, key_head, contract_last, preferred_element_ty...]
    all_to_all x4 -> x0, local copies, waits for them, and re-layouts: 5.49 us -> none  [the longest x1 1.64 us: on_device(): lax.all_to_all(q_old, 'head', split_axis=1, concat_axis=0, tiled=True)]
    gather x3 -> x0, local copies, waits for them, and re-layouts: 2.29 us -> none  [relocate(): jnp.take(candidates, selected, axis=0)]
  transfers between devices with their start and end apart: 24 -> 0, of which waited for: 13 -> 0; matrix products, arithmetic and copies ran while one was open for 8% -> 0% of each run, Pallas kernels for 0% -> 0%
where the time goes in v1:
time: 53.7 us; the launch traced here: 53.1 us
  Pallas kernels  48.2 us (90%)
  local copies, waits for them, and re-layouts  4.25 us (8%)
  between operations  0.65 us (1%)
    pallas_call x1, Pallas kernels, joint(): pl.pallas_call(functools.partial(joint_kernel, levels, pair, groups, memb...  48.2 us
    unnamed x10, local copies, waits for them, and re-layouts  4.25 us

profile of v1, /device:TPU:0, one launch (start us, length us, event | category | flops | bytes accessed | tf_op | source)
XLA Modules:
  0.0 53.1 jit_solution(8113692410691235243)
XLA Ops:
  0.6 48.2 %shard_map.93 = (bf16[224,512]{1,0:T(8,128)(2,1)}, bf16[224,512]{1,0:T(8,128)(2,1)}, bf16[224,256]{1,0:T(8,128)(2,1)}, bf16[224,256]{1,0:T(8,128)(2,1)}) custom-call(s32[9]{0:T(128)} %refs_0_.1, s32[9]{0:T(128)} %refs_1_.1, bf16[56,2048]{1,0:T(8,128)(2,1)} %refs_2_.1, bf16[56,1024]{1,0:T(8,128)(2,1)} %refs_3_.1, bf16[56,1024]{1,0:T(8,128)(2,1)} %refs_4_.1, ...), custom_call_target="tpu_custom_call" | custom-call | tf_op jit(solution)/shard_map/pallas_call | solution.py:549
  48.8 0.0 copy-start
  48.8 1.7 %copy.14 = bf16[224,512]{1,0:T(8,128)(2,1)} copy(bf16[224,512]{1,0:T(8,128)(2,1)} %get-tuple-element.8) | data formatting | bytes 458752
  50.5 0.0 copy-done
  50.5 0.0 copy-start.2
  50.5 0.7 %copy.15 = bf16[224,512]{1,0:T(8,128)(2,1)} copy(bf16[224,512]{1,0:T(8,128)(2,1)S(1)} %copy-done) | data formatting | bytes 458752
  51.2 0.3 copy-done.2
  51.5 0.0 copy-start.1
  51.5 0.6 %copy.16 = bf16[224,256]{1,0:T(8,128)(2,1)} copy(bf16[224,256]{1,0:T(8,128)(2,1)S(1)} %copy-done.2) | data formatting | bytes 229376
  52.1 0.3 copy-done.1
  52.4 0.6 %copy.17 = bf16[224,256]{1,0:T(8,128)(2,1)} copy(bf16[224,256]{1,0:T(8,128)(2,1)S(1)} %copy-done.1) | data formatting | bytes 229376
Async XLA Ops:
  48.8 1.7 %copy-start = (bf16[224,512]{1,0:T(8,128)(2,1)S(1)}, bf16[224,512]{1,0:T(8,128)(2,1)}, u32[]{:S(2)}) copy-start(bf16[224,512]{1,0:T(8,128)(2,1)} %get-tuple-element.9) | copy-start | bytes 688132
  50.5 1.0 %copy-start.2 = (bf16[224,256]{1,0:T(8,128)(2,1)S(1)}, bf16[224,256]{1,0:T(8,128)(2,1)}, u32[]{:S(2)}) copy-start(bf16[224,256]{1,0:T(8,128)(2,1)} %get-tuple-element.10) | copy-start | bytes 344068
  51.5 0.9 %copy-start.1 = (bf16[224,256]{1,0:T(8,128)(2,1)S(1)}, bf16[224,256]{1,0:T(8,128)(2,1)}, u32[]{:S(2)}) copy-start(bf16[224,256]{1,0:T(8,128)(2,1)} %get-tuple-element.11) | copy-start | bytes 344068

commit v2 on v1

--- a/solution.py
+++ b/solution.py
@@ -200,10 +200,9 @@
 
 
 def joint_kernel(levels, pair, groups, members, *refs):
-    (old_offsets, new_offsets, q_in, k_in, v_in, d_in, attn_out, dq_out, dk_out, dv_out,
+    (old_offsets, q_in, k_in, v_in, d_in, row_ext, dk_ext, dv_ext,
      kv_chunks, qd_chunks, wide, kv_wide, qd_wide, kv_halo, qd_halo, keys, values, queries, grads,
-     probs, grad_probs, grad_send, grad_recv, grad_own, attn_t, dq_t, row_buf, grad_buf, row_ext,
-     grad_ext, in_send, in_recv, in_local, halo_send, halo_recv, cast_send, cast_recv, ret_send,
+     probs, grad_probs, grad_send, grad_recv, grad_own, attn_t, dq_t, row_buf, grad_buf, in_send, in_recv, in_local, halo_send, halo_recv, cast_send, cast_recv, ret_send,
      ret_recv, out_send, out_recv, out_local) = refs
     seq, column = lax.axis_index("seq"), lax.axis_index("head")
     level, part = seq // pair, seq % pair
@@ -303,43 +302,59 @@
         def _():
             send(*up, halo_send.at[kind, 0], halo_recv.at[kind, 0], at(level + 1, part, column)).start()
 
-        @pl.when(level > 0)
-        def _():
-            landed(dest.at[0], halo_recv.at[kind, 0])
-
-        @pl.when(level == 0)
-        def _():
-            dest[0] = jnp.zeros(dest.shape[1:], bf16)
-
-        @pl.when(level < levels - 1)
-        def _():
-            landed(dest.at[1], halo_recv.at[kind, 1])
-
-        @pl.when(level == levels - 1)
-        def _():
-            dest[1] = jnp.zeros(dest.shape[1:], bf16)
-
-        return jnp.concatenate([
-            source[pl.ds(slack, slack)] + dest[0],
-            source[pl.ds(2 * slack, rows - 2 * slack)],
-            source[pl.ds(rows, slack)] + dest[1],
-        ], axis=0)
+        def finish():
+            @pl.when(level > 0)
+            def _():
+                landed(dest.at[0], halo_recv.at[kind, 0])
+
+            @pl.when(level == 0)
+            def _():
+                dest[0] = jnp.zeros(dest.shape[1:], bf16)
+
+            @pl.when(level < levels - 1)
+            def _():
+                landed(dest.at[1], halo_recv.at[kind, 1])
+
+            @pl.when(level == levels - 1)
+            def _():
+                dest[1] = jnp.zeros(dest.shape[1:], bf16)
+
+            return jnp.concatenate([
+                source[pl.ds(slack, slack)] + dest[0],
+                source[pl.ds(2 * slack, rows - 2 * slack)],
+                source[pl.ds(rows, slack)] + dest[1],
+            ], axis=0)
+
+        return finish
 
     arrive((0, 1))
     spread(kv_chunks, kv_wide)
-    block = halo(0, kv_wide, kv_halo)
+    block = halo(0, kv_wide, kv_halo)()
     keys[level] = block[:, :HEAD_SIZE]
     values[level] = block[:, HEAD_SIZE:]
-    for kind, held in ((0, keys), (1, values)):
-        for step in range(1, levels):
-            @pl.when(level + step < levels)
-            def _():
-                send(held.at[level], held.at[level], cast_send.at[kind, step],
-                     cast_recv.at[kind, step], at(level + step, part, column)).start()
+
+    def forward(step):
+        @pl.when(level < levels - 1)
+        def _():
+            send(keys.at[level - step], keys.at[level - step], cast_send.at[0, step],
+                 cast_recv.at[0, step + 1], at(level + 1, part, column)).start()
+
+    forward(0)
+    if levels > 1:
+        @pl.when(level > 0)
+        def _():
+            landed(keys.at[level - 1], cast_recv.at[0, 1])
+            forward(1)
 
     arrive((2, 3))
     spread(qd_chunks, qd_wide)
-    block = halo(1, qd_wide, qd_halo)
+    finish = halo(1, qd_wide, qd_halo)
+    for step in range(1, levels):
+        @pl.when(level + step < levels)
+        def _():
+            send(values.at[level], values.at[level], cast_send.at[1, step],
+                 cast_recv.at[1, step], at(level + step, part, column)).start()
+    block = finish()
     for member in range(members):
         span = pl.ds(member * rows, rows)
         queries[span] = block[:, member * HEAD_SIZE:(member + 1) * HEAD_SIZE]
@@ -350,9 +365,10 @@
     lanes = members * rows
 
     def score_step(step, row_max):
-        @pl.when(step > 0)
+        @pl.when(step > 1)
         def _():
             landed(keys.at[level - step], cast_recv.at[0, step])
+            forward(step)
 
         score = lax.dot_general(keys[level - step], queries[...], nt, preferred_element_type=f32) * query_scale
         key_place = lax.broadcasted_iota(jnp.int32, (rows, rows), 0)
@@ -371,6 +387,25 @@
 
     row_total = lax.fori_loop(0, level + 1, weight_step, jnp.zeros((1, lanes), f32))
     inverse = 1.0 / row_total
+
+    def share(kind, low, term):
+        @pl.when(low < level)
+        def _():
+            grad_send[kind, low] = term.astype(bf16)
+            send(grad_send.at[kind, low], grad_recv.at[kind, level - low], ret_send.at[kind, level - low],
+                 ret_recv.at[kind, level - low], at(low, part, column)).start()
+
+        @pl.when(low == level)
+        def _():
+            grad_own[kind] = term
+
+    def prob_step(low, carry):
+        prob = probs[low] * inverse
+        probs[low] = prob
+        share(0, low, jnp.dot(prob.astype(bf16), grads[...], preferred_element_type=f32))
+        return carry
+
+    lax.fori_loop(0, level + 1, prob_step, 0)
     attn_t[...] = jnp.zeros_like(attn_t)
 
     def value_step(step, carry):
@@ -378,9 +413,8 @@
         def _():
             landed(values.at[level - step], cast_recv.at[1, step])
 
-        prob = probs[level - step] * inverse
-        probs[level - step] = prob
-        attn_t[...] += lax.dot_general(values[level - step], prob.astype(bf16), tn, preferred_element_type=f32)
+        prob = probs[level - step].astype(bf16)
+        attn_t[...] += lax.dot_general(values[level - step], prob, tn, preferred_element_type=f32)
         grad_probs[level - step] = lax.dot_general(values[level - step], grads[...], nt, preferred_element_type=f32)
         return carry
 
@@ -394,19 +428,7 @@
         prob = probs[low]
         change = (prob * (grad_probs[low] - delta) * query_scale).astype(bf16)
         dq_t[...] += lax.dot_general(keys[low], change, tn, preferred_element_type=f32)
-        dk = jnp.dot(change, queries[...], preferred_element_type=f32)
-        dv = jnp.dot(prob.astype(bf16), grads[...], preferred_element_type=f32)
-
-        @pl.when(low < level)
-        def _():
-            grad_send[low] = jnp.concatenate([dk, dv], axis=1).astype(bf16)
-            send(grad_send.at[low], grad_recv.at[level - low], ret_send.at[level - low],
-                 ret_recv.at[level - low], at(low, part, column)).start()
-
-        @pl.when(low == level)
-        def _():
-            grad_own[...] = jnp.concatenate([dk, dv], axis=1)
-
+        share(1, low, jnp.dot(change, queries[...], preferred_element_type=f32))
         return carry
 
     lax.fori_loop(0, level + 1, grad_step, 0)
@@ -447,7 +469,7 @@
             send(source.at[head_span], dest.at[part, tail_span], out_send.at[kind, pair + 1],
                  out_recv.at[kind, part, 2], at(level - 1, pair - 1, column)).start()
 
-    def take_in(kind, source, dest, place):
+    def take_in(kind, source, dest):
         for other in range(pair):
             take, put = routes(other)
 
@@ -487,26 +509,18 @@
         def _():
             left(source.at[head_span], out_send.at[kind, pair + 1])
 
-        first, end = new_offsets[seq], new_offsets[seq + 1]
-        slot = lax.broadcasted_iota(jnp.int32, (slots, slots), 0) + first
-        held = lax.broadcasted_iota(jnp.int32, (slots, slots), 1) + (seq * TOK_DEV - slack)
-        pick = jnp.where((slot == held) & (slot < end), 1.0, 0.0).astype(bf16)
-        for giver in range(pair):
-            placed = jnp.dot(pick, dest[giver], preferred_element_type=f32).astype(bf16)
-            for index, out in enumerate(place):
-                count = dest.shape[2] // 2
-                out[:, pl.ds(giver * count, count)] = placed[:, index * count:(index + 1) * count]
-
     hand_out(0, row_buf, row_ext)
-    for step in range(1, levels):
-        @pl.when(level + step < levels)
-        def _():
-            landed(grad_recv.at[step], ret_recv.at[step])
-            grad_own[...] += grad_recv[step].astype(f32)
-    grad_buf[...] = grad_own[...].astype(bf16)
-    hand_out(1, grad_buf, grad_ext)
-    take_in(0, row_buf, row_ext, (attn_out, dq_out))
-    take_in(1, grad_buf, grad_ext, (dk_out, dv_out))
+    for kind, dest in ((0, dv_ext), (1, dk_ext)):
+        for step in range(1, levels):
+            @pl.when(level + step < levels)
+            def _():
+                landed(grad_recv.at[kind, step], ret_recv.at[kind, step])
+                grad_own[kind] += grad_recv[kind, step].astype(f32)
+        grad_buf[kind] = grad_own[kind].astype(bf16)
+        hand_out(1 + kind, grad_buf.at[kind], dest)
+    take_in(0, row_buf, row_ext)
+    take_in(1, grad_buf.at[0], dv_ext)
+    take_in(2, grad_buf.at[1], dk_ext)
 
     for kind in range(4):
         for step in range(1, crowd):
@@ -520,14 +534,34 @@
         def _():
             left(source.at[pl.ds(rows + slack, slack)], halo_send.at[kind, 0])
     for step in range(1, levels):
-        for kind, held in ((0, keys), (1, values)):
-            @pl.when(level + step < levels)
-            def _():
-                left(held.at[level], cast_send.at[kind, step])
+        @pl.when(level + step < levels)
+        def _():
+            left(values.at[level], cast_send.at[1, step])
+
+        @pl.when((level < levels - 1) & (level >= step - 1))
+        def _():
+            left(keys.at[level - step + 1], cast_send.at[0, step - 1])
 
         @pl.when(level >= step)
         def _():
-            left(grad_send.at[level - step], ret_send.at[step])
+            for kind in range(2):
+                left(grad_send.at[kind, level - step], ret_send.at[kind, step])
+
+
+def place_kernel(new_offsets, row_ext, dk_ext, dv_ext, attn_out, dq_out, dk_out, dv_out):
+    seq = lax.axis_index("seq")
+    pair, slots, width = row_ext.shape
+    slack = (slots - TOK_DEV) // 2
+    first, end = new_offsets[seq], new_offsets[seq + 1]
+    slot = lax.broadcasted_iota(jnp.int32, (slots, slots), 0) + first
+    held = lax.broadcasted_iota(jnp.int32, (slots, slots), 1) + (seq * TOK_DEV - slack)
+    pick = jnp.where((slot == held) & (slot < end), 1.0, 0.0).astype(jnp.bfloat16)
+    for giver in range(pair):
+        for ext, outs in ((row_ext, (attn_out, dq_out)), (dk_ext, (dk_out,)), (dv_ext, (dv_out,))):
+            placed = jnp.dot(pick, ext[giver], preferred_element_type=jnp.float32).astype(jnp.bfloat16)
+            count = ext.shape[2] // len(outs)
+            for index, out in enumerate(outs):
+                out[:, pl.ds(giver * count, count)] = placed[:, index * count:(index + 1) * count]
 
 
 def joint(sequence, groups, q_old, k_old, value_old_layout, dout_old, old_offsets, new_offsets):
@@ -546,11 +580,12 @@
     smem = pl.BlockSpec(memory_space=pltpu.SMEM)
     anywhere = pl.BlockSpec(memory_space=pl.ANY)
     whole = pl.BlockSpec(memory_space=pltpu.VMEM)
-    return pl.pallas_call(
+    held = lambda count: jax.ShapeDtypeStruct((pair, slots, count), bf16)
+    landed = pl.pallas_call(
         functools.partial(joint_kernel, levels, pair, groups, members),
-        out_shape=(out(pair * width), out(pair * width), out(pair * HEAD_SIZE), out(pair * HEAD_SIZE)),
-        in_specs=[smem, smem, anywhere, anywhere, anywhere, anywhere],
-        out_specs=(whole,) * 4,
+        out_shape=(held(2 * width), held(HEAD_SIZE), held(HEAD_SIZE)),
+        in_specs=[smem, anywhere, anywhere, anywhere, anywhere],
+        out_specs=(whole,) * 3,
         scratch_shapes=[
             vmem((pair * groups, chunk, 2 * HEAD_SIZE), bf16),
             vmem((pair * groups, chunk, 2 * width), bf16),
@@ -565,23 +600,29 @@
             vmem((lanes, HEAD_SIZE), bf16),
             vmem((levels, rows, lanes), f32),
             vmem((levels, rows, lanes), f32),
-            vmem((levels, rows, 2 * HEAD_SIZE), bf16),
-            vmem((levels, rows, 2 * HEAD_SIZE), bf16),
-            vmem((rows, 2 * HEAD_SIZE), f32),
+            vmem((2, levels, rows, HEAD_SIZE), bf16),
+            vmem((2, levels, rows, HEAD_SIZE), bf16),
+            vmem((2, rows, HEAD_SIZE), f32),
             vmem((HEAD_SIZE, lanes), f32),
             vmem((HEAD_SIZE, lanes), f32),
             vmem((rows, 2 * width), bf16),
-            vmem((rows, 2 * HEAD_SIZE), bf16),
-            vmem((pair, slots, 2 * width), bf16),
-            vmem((pair, slots, 2 * HEAD_SIZE), bf16),
+            vmem((2, rows, HEAD_SIZE), bf16),
             dma((4, pair * groups)), dma((4, pair * groups)), dma((4,)),
             dma((2, 2)), dma((2, 2)),
             dma((2, levels)), dma((2, levels)),
-            dma((levels,)), dma((levels,)),
-            dma((2, pair + 2)), dma((2, pair, 3)), dma((2,)),
+            dma((2, levels)), dma((2, levels)),
+            dma((3, pair + 2)), dma((3, pair, 3)), dma((3,)),
         ],
-        compiler_params=pltpu.CompilerParams(collective_id=0, has_side_effects=True),
-    )(old_offsets, new_offsets, q_old, k_old, value_old_layout, dout_old)
+        compiler_params=pltpu.CompilerParams(
+            collective_id=0, has_side_effects=True, vmem_limit_bytes=24 << 20),
+    )(old_offsets, q_old, k_old, value_old_layout, dout_old)
+    return pl.pallas_call(
+        place_kernel,
+        out_shape=(out(pair * width), out(pair * width), out(pair * HEAD_SIZE), out(pair * HEAD_SIZE)),
+        in_specs=[smem] + [whole] * 3,
+        out_specs=(whole,) * 4,
+        compiler_params=pltpu.CompilerParams(vmem_limit_bytes=8 << 20),
+    )(new_offsets, *landed)
 
 
 def solution(mesh):

time: 53.7 us -> 52 us (0.968)
  Pallas kernels: 48.2 us -> 46.1 us
  local copies, waits for them, and re-layouts: 4.25 us -> 4.97 us
    pallas_call x1, Pallas kernels: 48.2 us -> 44.4 us  [joint(): pl.pallas_call(functools.partial(joint_kernel, levels, pair, groups, memb...]
    pallas_call x0 -> x1, Pallas kernels: none -> 1.72 us  [joint(): pl.pallas_call(place_kernel, out_shape=(out(pair * width), out(pair * wid...]
    unnamed x10 -> x12, local copies, waits for them, and re-layouts: 4.25 us -> 4.97 us
where the time goes in v2:
time: 52 us; the launch traced here: 51.8 us
  Pallas kernels  46.1 us (89%)
  local copies, waits for them, and re-layouts  4.97 us (10%)
  between operations  0.66 us (1%)
    pallas_call x1, Pallas kernels, joint(): pl.pallas_call(functools.partial(joint_kernel, levels, pair, groups, memb...  44.4 us
    unnamed x12, local copies, waits for them, and re-layouts  4.97 us
    pallas_call x1, Pallas kernels, joint(): pl.pallas_call(place_kernel, out_shape=(out(pair * width), out(pair * wid...  1.72 us

profile of v2, /device:TPU:0, one launch (start us, length us, event | category | flops | bytes accessed | tf_op | source)
XLA Modules:
  0.0 51.8 jit_solution(7012783228083962984)
XLA Ops:
  0.6 0.0 copy-start
  0.6 0.9 %copy-done = bf16[56,2048]{1,0:T(8,128)(2,1)S(1)} copy-done((bf16[56,2048]{1,0:T(8,128)(2,1)S(1)}, bf16[56,2048]{1,0:T(8,128)(2,1)}, u32[]{:S(2)}) %copy-start) | copy-done | bytes 229400
  1.6 0.0 copy-start.1
  1.6 0.9 %copy-done.1 = bf16[56,2048]{1,0:T(8,128)(2,1)S(1)} copy-done((bf16[56,2048]{1,0:T(8,128)(2,1)S(1)}, bf16[56,2048]{1,0:T(8,128)(2,1)}, u32[]{:S(2)}) %copy-start.1) | copy-done | bytes 229400
  2.5 0.0 copy-start.2
  2.5 0.9 %copy-done.2 = bf16[56,1024]{1,0:T(8,128)(2,1)S(1)} copy-done((bf16[56,1024]{1,0:T(8,128)(2,1)S(1)}, bf16[56,1024]{1,0:T(8,128)(2,1)}, u32[]{:S(2)}) %copy-start.2) | copy-done | bytes 114712
  3.4 0.0 copy-start.3
  3.4 0.9 %copy-done.3 = bf16[56,1024]{1,0:T(8,128)(2,1)S(1)} copy-done((bf16[56,1024]{1,0:T(8,128)(2,1)S(1)}, bf16[56,1024]{1,0:T(8,128)(2,1)}, u32[]{:S(2)}) %copy-start.3) | copy-done | bytes 114712
  4.3 0.0 copy-start.4
  4.3 0.7 %copy-done.4 = s32[9]{0:T(128)S(1)} copy-done((s32[9]{0:T(128)S(1)}, s32[9]{0:T(128)}, u32[]{:S(2)}) %copy-start.4) | copy-done | bytes 60
  5.0 44.4 %shard_map.93 = (bf16[2,224,512]{2,1,0:T(8,128)(2,1)S(1)}, bf16[2,224,128]{2,1,0:T(8,128)(2,1)S(1)}, bf16[2,224,128]{2,1,0:T(8,128)(2,1)S(1)}) custom-call(s32[9]{0:T(128)S(1)} %copy-done.4, bf16[56,2048]{1,0:T(8,128)(2,1)S(1)} %copy-done, bf16[56,1024]{1,0:T(8,128)(2,1)S(1)} %copy-done.2, bf16[56,1024]{1,0:T(8,128)(2,1)S(1)} %copy-done.3, ...), custom_call_target="tpu_custom_call" | custom-call | tf_op jit(solution)/shard_map/pallas_call | solution.py:584
  49.4 0.0 copy-start.5
  49.4 0.6 %copy-done.5 = s32[9]{0:T(128)S(1)} copy-done((s32[9]{0:T(128)S(1)}, s32[9]{0:T(128)}, u32[]{:S(2)}) %copy-start.5) | copy-done | bytes 60
  50.0 1.7 %shard_map.94 = (bf16[224,512]{1,0:T(8,128)(2,1)}, bf16[224,512]{1,0:T(8,128)(2,1)}, bf16[224,256]{1,0:T(8,128)(2,1)}, bf16[224,256]{1,0:T(8,128)(2,1)}) custom-call(s32[9]{0:T(128)S(1)} %copy-done.5, bf16[2,224,512]{2,1,0:T(8,128)(2,1)S(1)} %get-tuple-element.7.row_ext, bf16[2,224,128]{2,1,0:T(8,128)(2,1)S(1)} %get-tuple-element.8.dk_ext, ...), custom_call_target="tpu_custom_call" | custom-call | tf_op jit(solution)/shard_map/pallas_call | solution.py:619
Async XLA Ops:
  0.6 0.9 %copy-start = (bf16[56,2048]{1,0:T(8,128)(2,1)S(1)}, bf16[56,2048]{1,0:T(8,128)(2,1)}, u32[]{:S(2)}) copy-start(bf16[56,2048]{1,0:T(8,128)(2,1)} %refs_1_.1) | copy-start | bytes 688132
  1.6 0.9 %copy-start.1 = (bf16[56,2048]{1,0:T(8,128)(2,1)S(1)}, bf16[56,2048]{1,0:T(8,128)(2,1)}, u32[]{:S(2)}) copy-start(bf16[56,2048]{1,0:T(8,128)(2,1)} %refs_4_.1) | copy-start | bytes 688132
  2.5 0.9 %copy-start.2 = (bf16[56,1024]{1,0:T(8,128)(2,1)S(1)}, bf16[56,1024]{1,0:T(8,128)(2,1)}, u32[]{:S(2)}) copy-start(bf16[56,1024]{1,0:T(8,128)(2,1)} %refs_2_.1) | copy-start | bytes 344068
  3.4 0.9 %copy-start.3 = (bf16[56,1024]{1,0:T(8,128)(2,1)S(1)}, bf16[56,1024]{1,0:T(8,128)(2,1)}, u32[]{:S(2)}) copy-start(bf16[56,1024]{1,0:T(8,128)(2,1)} %refs_3_.1) | copy-start | bytes 344068
  4.3 0.7 %copy-start.4 = (s32[9]{0:T(128)S(1)}, s32[9]{0:T(128)}, u32[]{:S(2)}) copy-start(s32[9]{0:T(128)} %refs_0_.1) | copy-start | bytes 112
  49.4 0.7 %copy-start.5 = (s32[9]{0:T(128)S(1)}, s32[9]{0:T(128)}, u32[]{:S(2)}) copy-start(s32[9]{0:T(128)} %new_offsets.1) | copy-start | bytes 112

commit v3 on v2

--- a/solution.py
+++ b/solution.py
@@ -200,10 +200,10 @@
 
 
 def joint_kernel(levels, pair, groups, members, *refs):
-    (old_offsets, q_in, k_in, v_in, d_in, row_ext, dk_ext, dv_ext,
+    (offsets_in, targets_in, q_in, k_in, v_in, d_in, row_ext, dk_ext, dv_ext, pick_out, old_offsets, new_offsets,
      kv_chunks, qd_chunks, wide, kv_wide, qd_wide, kv_halo, qd_halo, keys, values, queries, grads,
      probs, grad_probs, grad_send, grad_recv, grad_own, attn_t, dq_t, row_buf, grad_buf, in_send, in_recv, in_local, halo_send, halo_recv, cast_send, cast_recv, ret_send,
-     ret_recv, out_send, out_recv, out_local) = refs
+     ret_recv, out_send, out_recv, out_local, table_sem) = refs
     seq, column = lax.axis_index("seq"), lax.axis_index("head")
     level, part = seq // pair, seq % pair
     crowd = pair * groups
@@ -231,6 +231,9 @@
     def left(src, ssem):
         send(src, src, ssem, ssem, here).wait_send()
 
+    tables = ((offsets_in, old_offsets), (targets_in, new_offsets))
+    for index, (src, dst) in enumerate(tables):
+        pltpu.make_async_copy(src, dst, table_sem.at[index]).start()
     barrier = pltpu.get_barrier_semaphore()
     for step in range(1, crowd):
         peer = lax.rem(me + step, crowd)
@@ -327,6 +330,12 @@
 
         return finish
 
+    for index, (src, dst) in enumerate(tables):
+        pltpu.make_async_copy(src, dst, table_sem.at[index]).wait()
+    first, end = new_offsets[seq], new_offsets[seq + 1]
+    slot = lax.broadcasted_iota(jnp.int32, (slots, slots), 0) + first
+    held = lax.broadcasted_iota(jnp.int32, (slots, slots), 1) + (seq * TOK_DEV - slack)
+    pick_out[...] = jnp.where((slot == held) & (slot < end), 1.0, 0.0).astype(bf16)
     arrive((0, 1))
     spread(kv_chunks, kv_wide)
     block = halo(0, kv_wide, kv_halo)()
@@ -548,17 +557,11 @@
                 left(grad_send.at[kind, level - step], ret_send.at[kind, step])
 
 
-def place_kernel(new_offsets, row_ext, dk_ext, dv_ext, attn_out, dq_out, dk_out, dv_out):
-    seq = lax.axis_index("seq")
-    pair, slots, width = row_ext.shape
-    slack = (slots - TOK_DEV) // 2
-    first, end = new_offsets[seq], new_offsets[seq + 1]
-    slot = lax.broadcasted_iota(jnp.int32, (slots, slots), 0) + first
-    held = lax.broadcasted_iota(jnp.int32, (slots, slots), 1) + (seq * TOK_DEV - slack)
-    pick = jnp.where((slot == held) & (slot < end), 1.0, 0.0).astype(jnp.bfloat16)
+def place_kernel(row_ext, dk_ext, dv_ext, pick, attn_out, dq_out, dk_out, dv_out):
+    pair = row_ext.shape[0]
     for giver in range(pair):
         for ext, outs in ((row_ext, (attn_out, dq_out)), (dk_ext, (dk_out,)), (dv_ext, (dv_out,))):
-            placed = jnp.dot(pick, ext[giver], preferred_element_type=jnp.float32).astype(jnp.bfloat16)
+            placed = jnp.dot(pick[...], ext[giver], preferred_element_type=jnp.float32).astype(jnp.bfloat16)
             count = ext.shape[2] // len(outs)
             for index, out in enumerate(outs):
                 out[:, pl.ds(giver * count, count)] = placed[:, index * count:(index + 1) * count]
@@ -577,16 +580,17 @@
     bf16, f32 = jnp.bfloat16, jnp.float32
     vmem, dma = pltpu.VMEM, pltpu.SemaphoreType.DMA
     out = lambda count: jax.ShapeDtypeStruct((slots, count), bf16)
-    smem = pl.BlockSpec(memory_space=pltpu.SMEM)
-    anywhere = pl.BlockSpec(memory_space=pl.ANY)
+    anywhere = pl.BlockSpec(memory_space=pltpu.HBM)
     whole = pl.BlockSpec(memory_space=pltpu.VMEM)
     held = lambda count: jax.ShapeDtypeStruct((pair, slots, count), bf16)
     landed = pl.pallas_call(
         functools.partial(joint_kernel, levels, pair, groups, members),
-        out_shape=(held(2 * width), held(HEAD_SIZE), held(HEAD_SIZE)),
-        in_specs=[smem, anywhere, anywhere, anywhere, anywhere],
-        out_specs=(whole,) * 3,
+        out_shape=(held(2 * width), held(HEAD_SIZE), held(HEAD_SIZE), out(slots)),
+        in_specs=[anywhere] * 6,
+        out_specs=(whole,) * 4,
         scratch_shapes=[
+            pltpu.SMEM(old_offsets.shape, jnp.int32),
+            pltpu.SMEM(new_offsets.shape, jnp.int32),
             vmem((pair * groups, chunk, 2 * HEAD_SIZE), bf16),
             vmem((pair * groups, chunk, 2 * width), bf16),
             vmem((rows + 2 * slack, 2 * width), f32),
@@ -611,18 +615,18 @@
             dma((2, 2)), dma((2, 2)),
             dma((2, levels)), dma((2, levels)),
             dma((2, levels)), dma((2, levels)),
-            dma((3, pair + 2)), dma((3, pair, 3)), dma((3,)),
+            dma((3, pair + 2)), dma((3, pair, 3)), dma((3,)), dma((2,)),
         ],
         compiler_params=pltpu.CompilerParams(
-            collective_id=0, has_side_effects=True, vmem_limit_bytes=24 << 20),
-    )(old_offsets, q_old, k_old, value_old_layout, dout_old)
+            collective_id=0, has_side_effects=True, vmem_limit_bytes=66400000),
+    )(old_offsets, new_offsets, q_old, k_old, value_old_layout, dout_old)
     return pl.pallas_call(
         place_kernel,
         out_shape=(out(pair * width), out(pair * width), out(pair * HEAD_SIZE), out(pair * HEAD_SIZE)),
-        in_specs=[smem] + [whole] * 3,
+        in_specs=[whole] * 4,
         out_specs=(whole,) * 4,
-        compiler_params=pltpu.CompilerParams(vmem_limit_bytes=8 << 20),
-    )(new_offsets, *landed)
+        compiler_params=pltpu.CompilerParams(vmem_limit_bytes=66400000),
+    )(*landed)
 
 
 def solution(mesh):

time: 52 us -> 48.1 us (0.925)
  local copies, waits for them, and re-layouts: 4.97 us -> 0 us
  Pallas kernels: 46.1 us -> 47.3 us
    unnamed x12 -> x0, local copies, waits for them, and re-layouts: 4.97 us -> none
    pallas_call x1, Pallas kernels: 1.72 us -> 2.31 us  [joint(): pl.pallas_call(place_kernel, out_shape=(out(pair * width), out(pair * wid...]
    pallas_call x1, Pallas kernels: 44.4 us -> 45 us  [joint(): pl.pallas_call(functools.partial(joint_kernel, levels, pair, groups, memb...]
where the time goes in v3:
time: 48.1 us; the launch traced here: 47.9 us
  Pallas kernels  47.3 us (98%)
  between operations  0.64 us (1%)
    pallas_call x1, Pallas kernels, joint(): pl.pallas_call(functools.partial(joint_kernel, levels, pair, groups, memb...  45 us
    pallas_call x1, Pallas kernels, joint(): pl.pallas_call(place_kernel, out_shape=(out(pair * width), out(pair * wid...  2.31 us

profile of v3, /device:TPU:0, one launch (start us, length us, event | category | flops | bytes accessed | tf_op | source)
XLA Modules:
  0.0 47.9 jit_solution(9894183133949283352)
XLA Ops:
  0.6 45.0 %shard_map.93 = (bf16[2,224,512]{2,1,0:T(8,128)(2,1)}, bf16[2,224,128]{2,1,0:T(8,128)(2,1)}, bf16[2,224,128]{2,1,0:T(8,128)(2,1)}, bf16[224,224]{1,0:T(8,128)(2,1)}) custom-call(s32[9]{0:T(128)} %refs_0_.1, s32[9]{0:T(128)} %refs_1_.1, bf16[56,2048]{1,0:T(8,128)(2,1)} %refs_2_.1, bf16[56,1024]{1,0:T(8,128)(2,1)} %refs_3_.1, bf16[56,1024]{1,0:T(8,128)(2,1)} %refs_4_.1, ...), custom_call_target="tpu_custom_call" | custom-call | tf_op jit(solution)/shard_map/pallas_call | solution.py:586
  45.6 2.3 %shard_map.94 = (bf16[224,512]{1,0:T(8,128)(2,1)}, bf16[224,512]{1,0:T(8,128)(2,1)}, bf16[224,256]{1,0:T(8,128)(2,1)}, bf16[224,256]{1,0:T(8,128)(2,1)}) custom-call(bf16[2,224,512]{2,1,0:T(8,128)(2,1)} %get-tuple-element.8.row_ext, bf16[2,224,128]{2,1,0:T(8,128)(2,1)} %get-tuple-element.9.dk_ext, bf16[2,224,128]{2,1,0:T(8,128)(2,1)} %get-tuple-element.10.dv_ext, ...), custom_call_target="tpu_custom_call" | custom-call | tf_op jit(solution)/shard_map/pallas_call | solution.py:623
